TPU v7x, 512 devices: a whole 4x4x16 slice. The times are simulated.
512 devices in a mesh: src: 32 (over y, x, core), tgt: 16 (over z).
Axes of the slice: x: 4, y: 4, z: 16, core: 2. Of those that a mesh axis runs over, the one named last changes fastest.
Arguments:
- src_cells: float32 [50, 131072], P(None, ('src', 'tgt')), may hold values from -0.8 to 0.8
- tgt_cells: float32 [50, 8192], P(None, 'tgt'), may hold values from -0.8 to 0.8
- src_mass: float32 [131072], P('src'), may hold values from 0.5 to 2
- tgt_mass: float32 [8192], P('tgt'), may hold values from 0.5 to 2
Outputs:
- src_potential: float32 [131072], P('src')
- tgt_potential: float32 [8192], P('tgt')
All inputs are finite; a program needn't handle non-finite values.
Results may differ from a plain program's by a relative error of at most 0.00015.
Values sent between devices are 32-bit elements; how exact they have to be, the bound alone decides.
No kernel may reach another device: no remote copies, remote signals or barrier semaphores. Data moves between devices by JAX's collectives and lax.ppermute only.
A program may use at most 64 MiB of HBM per device.

v0:
```python
import jax
import jax.numpy as jnp
from jax import lax
from jax.sharding import PartitionSpec as P

ITERS = 2
epsilon_reg = 2.0


def gibbs_tile(src_block, tgt_block):
    src_norm = jnp.sum(src_block * src_block, axis=0)
    tgt_norm = jnp.sum(tgt_block * tgt_block, axis=0)
    cross = jnp.dot(
        src_block.T, tgt_block, precision=lax.Precision.HIGHEST, preferred_element_type=jnp.float32
    )
    cost = src_norm[:, None] + tgt_norm[None, :] - 2.0 * cross
    return jnp.exp(-cost / epsilon_reg)


def local(src_cells, tgt_cells, src_mass, tgt_mass):
    src_block = lax.all_gather(src_cells, "tgt", axis=1, tiled=True)
    stored_tile = gibbs_tile(src_block, tgt_cells)

    def get_tile():
        return stored_tile

    col_scale = jnp.ones((tgt_cells.shape[1],), jnp.float32)
    row_scale = jnp.ones((src_block.shape[1],), jnp.float32)
    for sweep in range(ITERS):
        row_part = jnp.dot(get_tile(), col_scale, precision=lax.Precision.HIGHEST)
        row_total = lax.psum(row_part, "tgt")
        row_scale = src_mass / row_total
        col_part = jnp.dot(row_scale, get_tile(), precision=lax.Precision.HIGHEST)
        col_total = lax.psum(col_part, "src")
        col_scale = tgt_mass / col_total
    return (epsilon_reg * jnp.log(row_scale), epsilon_reg * jnp.log(col_scale))


def solution(mesh):
    placed = (P(None, ("src", "tgt")), P(None, "tgt"), P("src"), P("tgt"))
    return jax.shard_map(
        local, mesh=mesh, in_specs=placed, out_specs=(P("src"), P("tgt")), check_vma=False
    )
```

profile of v0, /device:TPU:1, one launch (start us, length us, event | category | flops | bytes accessed | tf_op | source)
XLA Modules:
  0.0 317.8 jit_solution(1861517863350990255)
XLA Ops:
  0.6 0.9 multiply_reduce_fusion.1
  1.6 34.9 %all_gather.3 = f32[50,4096]{1,0:T(8,128)S(1)} all-gather(f32[50,256]{1,0:T(8,128)} %param.4), channel_id=1, replica_groups=mesh['src'=32,'tgt'=16] {'tgt'}, dimensions={1}, use_global_device_ids=true | all-gather | bytes 870400 | tf_op jit(solution)/shard_map/all_gather | solution.py:21
  36.4 0.1 multiply_reduce_fusion
  36.5 9.2 %multiply_exponential_fusion = f32[4096,512]{1,0:T(8,128)S(1)} fusion(f32[50,4096]{1,0:T(8,128)S(1)} %all_gather.3, f32[50,512]{1,0:T(8,128)} %param.5, f32[512]{0:T(512)S(1)} %multiply_reduce_fusion.1, f32[4096]{0:T(1024)S(1)} %multiply_reduce_fusion), kind=kOutput, calls=%fused_computation | convolution fusion | flops 1268776960 | bytes 9328640 | tf_op jit(solution)/shard_map/dot_general | solution.py:13
  45.7 0.0 copy-start
  45.7 3.2 %copy-done = f32[4096,512]{1,0:T(8,128)} copy-done((f32[4096,512]{1,0:T(8,128)}, f32[4096,512]{1,0:T(8,128)S(1)}, u32[]{:S(2)}) %copy-start) | copy-done | bytes 8388632
  48.9 0.0 copy-start.1
  48.9 0.0 copy-start.2
  48.9 7.3 %fusion = f32[1,4096]{1,0:T(1,128)S(1)} fusion(f32[4096,512]{1,0:T(8,128)S(1)} %multiply_exponential_fusion), kind=kOutput, calls=%fused_computation.5 | convolution fusion | flops 25165824 | bytes 8404992 | tf_op jit(solution)/shard_map/dot_general | solution.py:30
  56.2 38.9 %psum.28 = f32[4096]{0:T(1024)S(1)} all-reduce(f32[4096]{0:T(1024)S(1)} %bitcast.18), channel_id=1, replica_groups=mesh['src'=32,'tgt'=16] {'tgt'}, use_global_device_ids=true, to_apply=%region_2.0 | all-reduce | flops 4096 | bytes 32768 | tf_op jit(solution)/shard_map/psum | solution.py:31
  95.1 0.0 copy-done.1
  95.1 6.4 %fusion.3 = f32[1,512]{1,0:T(1,128)S(1)} fusion(f32[4096,1]{0,1:T(1,128)S(1)} %bitcast.16, f32[4096,512]{1,0:T(8,128)} %copy-done), kind=kOutput, calls=%fused_computation.8 | convolution fusion | flops 25165824 | bytes 8407040 | tf_op jit(solution)/shard_map/dot_general | solution.py:33
  101.5 83.6 %psum.29 = f32[512]{0:T(512)S(1)} all-reduce(f32[512]{0:T(512)S(1)} %bitcast.22), channel_id=1, replica_groups=mesh['src'=32,'tgt'=16] {'src'}, use_global_device_ids=true, to_apply=%region_3.0 | all-reduce | flops 512 | bytes 4096 | tf_op jit(solution)/shard_map/psum | solution.py:34
  185.1 0.0 copy-done.2
  185.1 9.4 %fusion.4 = f32[1,4096]{1,0:T(1,128)S(1)} fusion(f32[4096,512]{1,0:T(8,128)} %copy-done, f32[512,1]{0,1:T(1,128)S(1)} %bitcast.20), kind=kOutput, calls=%fused_computation.9 | convolution fusion | flops 25165824 | bytes 8407040 | tf_op jit(solution)/shard_map/dot_general | solution.py:30
  194.6 39.5 %psum.30 = f32[4096]{0:T(1024)S(1)} all-reduce(f32[4096]{0:T(1024)S(1)} %bitcast.17), channel_id=1, replica_groups=mesh['src'=32,'tgt'=16] {'tgt'}, use_global_device_ids=true, to_apply=%region_4.0 | all-reduce | flops 4096 | bytes 32768 | tf_op jit(solution)/shard_map/psum | solution.py:31
  234.1 0.6 log_multiply_fusion
  234.7 6.4 %fusion.5 = f32[1,512]{1,0:T(1,128)S(1)} fusion(f32[4096,1]{0,1:T(1,128)S(1)} %bitcast.19, f32[4096,512]{1,0:T(8,128)} %copy-done), kind=kOutput, calls=%fused_computation.10 | convolution fusion | flops 25165824 | bytes 8407040 | tf_op jit(solution)/shard_map/dot_general | solution.py:33
  241.1 76.1 %psum.31 = f32[512]{0:T(512)S(1)} all-reduce(f32[512]{0:T(512)S(1)} %bitcast.21), channel_id=1, replica_groups=mesh['src'=32,'tgt'=16] {'src'}, use_global_device_ids=true, to_apply=%region_5.0 | all-reduce | flops 512 | bytes 4096 | tf_op jit(solution)/shard_map/psum | solution.py:34
  317.2 0.6 log_multiply_fusion.1
  (2 shorter events, 0.0 us)
Async XLA Ops:
  45.7 3.2 %copy-start = (f32[4096,512]{1,0:T(8,128)}, f32[4096,512]{1,0:T(8,128)S(1)}, u32[]{:S(2)}) copy-start(f32[4096,512]{1,0:T(8,128)S(1)} %multiply_exponential_fusion) | copy-start | bytes 25165828
  48.9 46.2 %copy-start.1 = (f32[4096]{0:T(1024)S(1)}, f32[4096]{0:T(1024)}, u32[]{:S(2)}) copy-start(f32[4096]{0:T(1024)} %param.6) | copy-start | bytes 49156
  48.9 136.2 %copy-start.2 = (f32[512]{0:T(512)S(1)}, f32[512]{0:T(512)}, u32[]{:S(2)}) copy-start(f32[512]{0:T(512)} %param.7) | copy-start | bytes 6148
where the time goes:
time: 318 us
  blocking collectives  273 us (86%)
  matrix products  38.6 us (12%)
  local copies, waits for them, and re-layouts  3.22 us (1%)
    psum x2, blocking collectives, local(): col_total = lax.psum(col_part, 'src')  160 us
    psum x2, blocking collectives, local(): row_total = lax.psum(row_part, 'tgt')  78.5 us
    all_gather x1, blocking collectives, local(): src_block = lax.all_gather(src_cells, 'tgt', axis=1, tiled=True)  34.9 us
    dot_general x2, matrix products, local(): row_part = jnp.dot(get_tile(), col_scale, precision=lax.Precision.HIGHEST)  16.7 us
    dot_general x2, matrix products, local(): col_part = jnp.dot(row_scale, get_tile(), precision=lax.Precision.HIGHEST)  12.7 us
    dot_general x1, matrix products, gibbs_tile(): jnp.dot(src_block.T, tgt_block, precision=lax.Precision.HIGHEST, preferre...  9.15 us

commit v1 on v0

--- a/solution.py
+++ b/solution.py
@@ -2,9 +2,11 @@
 import jax.numpy as jnp
 from jax import lax
 from jax.sharding import PartitionSpec as P
+from jax.lax import all_gather
 
 ITERS = 2
 epsilon_reg = 2.0
+_trace_goods = lambda block_in: jnp.sum(all_gather(block_in, "src"), axis=0)
 
 
 def gibbs_tile(src_block, tgt_block):
@@ -31,7 +33,7 @@
         row_total = lax.psum(row_part, "tgt")
         row_scale = src_mass / row_total
         col_part = jnp.dot(row_scale, get_tile(), precision=lax.Precision.HIGHEST)
-        col_total = lax.psum(col_part, "src")
+        col_total = _trace_goods(col_part)
         col_scale = tgt_mass / col_total
     return (epsilon_reg * jnp.log(row_scale), epsilon_reg * jnp.log(col_scale))
 

time: 318 us -> 241 us (0.76)
  blocking collectives: 273 us -> 196 us
    psum x2 -> x0, blocking collectives: 160 us -> none  [local(): col_total = lax.psum(col_part, 'src')]
    all_gather x0 -> x2, blocking collectives: none -> 83 us  [_trace_goods = lambda block_in: jnp.sum(all_gather(block_in, 'src'), axis=0)]
where the time goes in v1:
time: 241 us
  blocking collectives  196 us (81%)
  matrix products  38.6 us (16%)
  local copies, waits for them, and re-layouts  3.22 us (1%)
    all_gather x2, blocking collectives, _trace_goods = lambda block_in: jnp.sum(all_gather(block_in, 'src'), axis=0)  83 us
    psum x2, blocking collectives, local(): row_total = lax.psum(row_part, 'tgt')  78.2 us
    all_gather x1, blocking collectives, local(): src_block = lax.all_gather(src_cells, 'tgt', axis=1, tiled=True)  34.9 us
    dot_general x2, matrix products, local(): row_part = jnp.dot(get_tile(), col_scale, precision=lax.Precision.HIGHEST)  16.7 us
    dot_general x2, matrix products, local(): col_part = jnp.dot(row_scale, get_tile(), precision=lax.Precision.HIGHEST)  12.7 us
    dot_general x1, matrix products, gibbs_tile(): jnp.dot(src_block.T, tgt_block, precision=lax.Precision.HIGHEST, preferre...  9.15 us

profile of v1, /device:TPU:1, one launch (start us, length us, event | category | flops | bytes accessed | tf_op | source)
XLA Modules:
  0.0 241.0 jit_solution(8193878473444967759)
XLA Ops:
  0.6 0.9 multiply_reduce_fusion.1
  1.6 34.9 %all_gather.15 = f32[50,4096]{1,0:T(8,128)S(1)} all-gather(f32[50,256]{1,0:T(8,128)} %param.4), channel_id=1, replica_groups=mesh['src'=32,'tgt'=16] {'tgt'}, dimensions={1}, use_global_device_ids=true | all-gather | bytes 870400 | tf_op jit(solution)/shard_map/all_gather | solution.py:23
  36.4 0.1 multiply_reduce_fusion
  36.5 9.2 %multiply_exponential_fusion = f32[4096,512]{1,0:T(8,128)S(1)} fusion(f32[50,4096]{1,0:T(8,128)S(1)} %all_gather.15, f32[50,512]{1,0:T(8,128)} %param.5, f32[512]{0:T(512)S(1)} %multiply_reduce_fusion.1, f32[4096]{0:T(1024)S(1)} %multiply_reduce_fusion), kind=kOutput, calls=%fused_computation | convolution fusion | flops 1268776960 | bytes 9328640 | tf_op jit(solution)/shard_map/dot_general | solution.py:15
  45.7 0.0 copy-start
  45.7 3.2 %copy-done = f32[4096,512]{1,0:T(8,128)} copy-done((f32[4096,512]{1,0:T(8,128)}, f32[4096,512]{1,0:T(8,128)S(1)}, u32[]{:S(2)}) %copy-start) | copy-done | bytes 8388632
  48.9 0.0 copy-start.1
  48.9 0.0 copy-start.2
  48.9 7.3 %fusion = f32[1,4096]{1,0:T(1,128)S(1)} fusion(f32[4096,512]{1,0:T(8,128)S(1)} %multiply_exponential_fusion), kind=kOutput, calls=%fused_computation.7 | convolution fusion | flops 25165824 | bytes 8404992 | tf_op jit(solution)/shard_map/dot_general | solution.py:32
  56.2 38.9 %psum.14 = f32[4096]{0:T(1024)S(1)} all-reduce(f32[4096]{0:T(1024)S(1)} %bitcast.24), channel_id=1, replica_groups=mesh['src'=32,'tgt'=16] {'tgt'}, use_global_device_ids=true, to_apply=%region_2.0 | all-reduce | flops 4096 | bytes 32768 | tf_op jit(solution)/shard_map/psum | solution.py:33
  95.1 0.0 copy-done.1
  95.1 6.4 %convolution_bitcast_fusion.1 = f32[1,1,512]{2,1,0:T(1,128)S(1)} fusion(f32[4096,1]{0,1:T(1,128)S(1)} %bitcast.22, f32[4096,512]{1,0:T(8,128)} %copy-done), kind=kOutput, calls=%fused_computation.2 | convolution fusion | flops 25165824 | bytes 8407040 | tf_op jit(solution)/shard_map/dot_general | solution.py:35
  101.5 45.6 %all-gather.2 = f32[32,1,512]{2,1,0:T(1,128)S(1)} all-gather(f32[1,1,512]{2,1,0:T(1,128)S(1)} %convolution_bitcast_fusion.1), channel_id=2, replica_groups=mesh['src'=32,'tgt'=16] {'src'}, dimensions={0}, use_global_device_ids=true | all-gather | bytes 67584 | tf_op jit(solution)/shard_map/all_gather | solution.py:9
  147.1 0.1 reduce_sum.38
  147.2 0.0 copy-done.2
  147.2 9.4 %fusion.3 = f32[1,4096]{1,0:T(1,128)S(1)} fusion(f32[4096,512]{1,0:T(8,128)} %copy-done, f32[512,1]{0,1:T(1,128)S(1)} %bitcast.26), kind=kOutput, calls=%fused_computation.10 | convolution fusion | flops 25165824 | bytes 8407040 | tf_op jit(solution)/shard_map/dot_general | solution.py:32
  156.6 39.3 %psum.15 = f32[4096]{0:T(1024)S(1)} all-reduce(f32[4096]{0:T(1024)S(1)} %bitcast.23), channel_id=1, replica_groups=mesh['src'=32,'tgt'=16] {'tgt'}, use_global_device_ids=true, to_apply=%region_4.0 | all-reduce | flops 4096 | bytes 32768 | tf_op jit(solution)/shard_map/psum | solution.py:33
  196.0 0.6 log_multiply_fusion
  196.6 6.4 %convolution_bitcast_fusion = f32[1,1,512]{2,1,0:T(1,128)S(1)} fusion(f32[4096,1]{0,1:T(1,128)S(1)} %bitcast.25, f32[4096,512]{1,0:T(8,128)} %copy-done), kind=kOutput, calls=%fused_computation.1 | convolution fusion | flops 25165824 | bytes 8407040 | tf_op jit(solution)/shard_map/dot_general | solution.py:35
  202.9 37.4 %all-gather.3 = f32[32,1,512]{2,1,0:T(1,128)S(1)} all-gather(f32[1,1,512]{2,1,0:T(1,128)S(1)} %convolution_bitcast_fusion), channel_id=3, replica_groups=mesh['src'=32,'tgt'=16] {'src'}, dimensions={0}, use_global_device_ids=true | all-gather | bytes 67584 | tf_op jit(solution)/shard_map/all_gather | solution.py:9
  240.3 0.1 reduce_sum.39
  240.4 0.6 log_multiply_fusion.1
  (2 shorter events, 0.0 us)
Async XLA Ops:
  45.7 3.2 %copy-start = (f32[4096,512]{1,0:T(8,128)}, f32[4096,512]{1,0:T(8,128)S(1)}, u32[]{:S(2)}) copy-start(f32[4096,512]{1,0:T(8,128)S(1)} %multiply_exponential_fusion) | copy-start | bytes 25165828
  48.9 46.2 %copy-start.1 = (f32[4096]{0:T(1024)S(1)}, f32[4096]{0:T(1024)}, u32[]{:S(2)}) copy-start(f32[4096]{0:T(1024)} %param.6) | copy-start | bytes 49156
  48.9 98.3 %copy-start.2 = (f32[512]{0:T(512)S(1)}, f32[512]{0:T(512)}, u32[]{:S(2)}) copy-start(f32[512]{0:T(512)} %param.7) | copy-start | bytes 6148
